TPU v7x, 32 devices: a whole 2x2x4 slice. The times are simulated.
32 devices in a mesh: dp: 8 (over z, y), mp: 4 (over x, core).
Axes of the slice: x: 2, y: 2, z: 4, core: 2. Of those that a mesh axis runs over, the one named last changes fastest.
Arguments:
- output_gradient: bfloat16 [1536, 3584], P('dp', 'mp'), may hold values from -6 to 6
- gate_preactivation: bfloat16 [1536, 9984], P('dp', 'mp'), may hold values from -8 to 8
- up_preactivation: bfloat16 [1536, 9984], P('dp', 'mp'), may hold values from -6 to 6
- down_weight: bfloat16 [9984, 3584], P('mp'), may hold values from -0.0625 to 0.0625
- adapter_first: bfloat16 [9984, 96], P('mp'), may hold values from -0.0625 to 0.0625
- adapter_second: bfloat16 [96, 3584], replicated, may hold values from -0.09375 to 0.09375
- plan: int32 [192], P('dp'), may hold values from 0 to 7, as said below
Outputs:
- grad_gate: bfloat16 [1536, 9984], P('dp', 'mp')
- grad_up: bfloat16 [1536, 9984], P('dp', 'mp')
- grad_a: float32 [4, 2496, 96], P('mp', 'dp')
- grad_b: float32 [96, 3584], P('dp')
Inputs may be any that keep to these rules, and one draw needn't show every extreme that they name: Every owner 0 to 7 is named by exactly 24 blocks; of the 24 blocks of one device (plan rows of one index of dp) at most 3 name the same owner, and in every draw some device's blocks name one owner exactly 3 times.
All inputs are finite; a program needn't handle non-finite values.
Results may differ from a plain program's by a relative error of at most 0.005.
Values may be sent and summed in bfloat16 or wider, within the bound.
No kernel may reach another device: no remote copies, remote signals or barrier semaphores. Data moves between devices by JAX's collectives and lax.ppermute only.
A program may use at most 64 MiB of HBM per device.

v0:
```python
import jax
import jax.numpy as jnp
from jax import lax
from jax.sharding import PartitionSpec as P


def body(
    output_gradient,
    gate_preactivation,
    up_preactivation,
    down_weight,
    adapter_first,
    adapter_second,
    plan,
):
    groups = lax.axis_size("dp")
    owned = plan.shape[0]
    capacity = -(-owned // groups)
    tokens_here = output_gradient.shape[0]
    feature_cols = output_gradient.shape[1]
    block_width = tokens_here // owned * feature_cols
    slot_count = groups * capacity
    positions = jnp.arange(owned, dtype=jnp.int32)
    earlier = (plan[None, :] == plan[:, None]) & (positions[None, :] < positions[:, None])
    target = plan * capacity + jnp.sum(earlier.astype(jnp.int32), axis=1)
    sending = target[None, :] == jnp.arange(slot_count, dtype=jnp.int32)[:, None]
    outgoing = jnp.dot(
        sending.astype(jnp.bfloat16),
        output_gradient.reshape(owned, block_width),
        preferred_element_type=jnp.float32,
    ).astype(jnp.bfloat16)
    filled = jnp.sum(sending.astype(jnp.float32), axis=1).astype(jnp.bfloat16)
    arrived, present = (
        lax.all_to_all(outgoing, "dp", split_axis=0, concat_axis=0, tiled=True),
        lax.all_to_all(filled, "dp", split_axis=0, concat_axis=0, tiled=True),
    )
    present_flag = present.astype(jnp.int32)
    ranking = jnp.cumsum(present_flag) - 1
    keeping = (ranking[None, :] == positions[:, None]) & (present_flag[None, :] > 0)
    packed_tokens = (
        jnp.dot(keeping.astype(jnp.bfloat16), arrived, preferred_element_type=jnp.float32)
        .astype(jnp.bfloat16)
        .reshape(tokens_here, feature_cols)
    )
    feature_rows = lax.all_gather(packed_tokens, "mp", axis=1, tiled=True)
    gate_vals = gate_preactivation.astype(jnp.float32)
    up_vals = up_preactivation.astype(jnp.float32)
    sigmoid_gate = jax.nn.sigmoid(gate_vals)
    silu_gate = gate_vals * sigmoid_gate
    hidden_units = (silu_gate * up_vals).astype(jnp.bfloat16)
    low_rank_piece = jnp.dot(hidden_units, adapter_first, preferred_element_type=jnp.float32)
    low_rank_rows = lax.psum(low_rank_piece, "mp").astype(jnp.bfloat16)
    passed_through = lax.dot_general(
        feature_rows, adapter_second, (((1,), (1,)), ((), ())), preferred_element_type=jnp.float32
    ).astype(jnp.bfloat16)
    grad_a_rows = lax.psum_scatter(
        lax.dot_general(
            hidden_units,
            passed_through,
            (((0,), (0,)), ((), ())),
            preferred_element_type=jnp.float32,
        ),
        "dp",
        scatter_dimension=0,
        tiled=True,
    )
    part_rows = lax.psum_scatter(
        lax.dot_general(
            low_rank_rows,
            packed_tokens,
            (((0,), (0,)), ((), ())),
            preferred_element_type=jnp.float32,
        ),
        "dp",
        scatter_dimension=0,
        tiled=True,
    )
    grad_b_rows = lax.all_gather(part_rows, "mp", axis=1, tiled=True)
    hidden_gradient = lax.dot_general(
        feature_rows, down_weight, (((1,), (1,)), ((), ())), preferred_element_type=jnp.float32
    )
    hidden_gradient = hidden_gradient + lax.dot_general(
        passed_through, adapter_first, (((1,), (1,)), ((), ())), preferred_element_type=jnp.float32
    )
    grad_gate = (
        hidden_gradient * up_vals * sigmoid_gate * (1.0 + gate_vals * (1.0 - sigmoid_gate))
    ).astype(jnp.bfloat16)
    grad_up = (hidden_gradient * silu_gate).astype(jnp.bfloat16)
    return (grad_gate, grad_up, grad_a_rows[None], grad_b_rows)


def solution(mesh):
    return jax.shard_map(
        body,
        mesh=mesh,
        in_specs=(
            P("dp", "mp"),
            P("dp", "mp"),
            P("dp", "mp"),
            P("mp", None),
            P("mp", None),
            P(),
            P("dp"),
        ),
        out_specs=(P("dp", "mp"), P("dp", "mp"), P("mp", "dp", None), P("dp", None)),
        check_vma=False,
    )
```

profile of v0, /device:TPU:0, one launch (start us, length us, event | category | flops | bytes accessed | tf_op | source)
XLA Modules:
  0.0 165.8 jit_solution(9476661914861650010)
XLA Ops:
  7.2 0.9 convert_reduce_fusion.1
  8.1 0.7 multiply_add_fusion
  8.8 0.1 convert_reduce_fusion
  8.9 0.7 convert_element_type.87
  9.6 7.3 %all-to-all-start = ((bf16[8,3,1]{1,2,0:T(2,128)(2,1)}), bf16[8,3,1]{1,2,0:T(2,128)(2,1)S(1)}, u32[]{:S(2)}, u32[]{:S(2)}) async-start(bf16[8,3,1]{1,2,0:T(2,128)(2,1)} %convert_element_type.87), calls=%async_computation | async-start | bytes 8192 | tf_op jit(solution)/shard_map/all_to_all | solution.py:35
  16.9 1.1 reshape.77
  18.0 0.2 convolution_convert_fusion.1
  18.3 1.0 all_to_all.13
  19.2 4.1 %all-to-all-done = bf16[8,3,1]{1,2,0:T(2,128)(2,1)S(1)} async-done(((bf16[8,3,1]{1,2,0:T(2,128)(2,1)}), bf16[8,3,1]{1,2,0:T(2,128)(2,1)S(1)}, u32[]{:S(2)}, u32[]{:S(2)}) %all-to-all-start) | async-done | bytes 80 | tf_op jit(solution)/shard_map/all_to_all | solution.py:35
  23.3 3.5 %all-to-all-start.1 = ((bf16[8,3,7168]{2,1,0:T(4,128)(2,1)}), bf16[8,3,7168]{2,1,0:T(4,128)(2,1)S(1)}, u32[]{:S(2)}, u32[]{:S(2)}) async-start(bf16[8,3,7168]{2,1,0:T(4,128)(2,1)} %all_to_all.13), calls=%async_computation.1 | async-start | bytes 917504 | tf_op jit(solution)/shard_map/all_to_all | solution.py:34
  27.1 0.1 add_reduce_fusion
  27.2 11.4 %all-to-all-done.1 = bf16[8,3,7168]{2,1,0:T(4,128)(2,1)S(1)} async-done(((bf16[8,3,7168]{2,1,0:T(4,128)(2,1)}), bf16[8,3,7168]{2,1,0:T(4,128)(2,1)S(1)}, u32[]{:S(2)}, u32[]{:S(2)}) %all-to-all-start.1) | async-done | bytes 344096 | tf_op jit(solution)/shard_map/all_to_all | solution.py:34
  38.6 0.3 all_to_all.15
  38.9 0.2 convolution_convert_fusion
  39.2 0.9 reshape.78
  40.1 17.7 %all-gather.2.cloned.1.call-done = bf16[192,3584]{1,0:T(8,128)(2,1)} async-done(((bf16[192,896]{1,0:T(8,128)(2,1)}), bf16[192,3584]{1,0:T(8,128)(2,1)}) %all-gather.2.cloned.1.call-update) | async-done | bytes 1376272 | tf_op jit(solution)/shard_map/all_gather | solution.py:45
  57.9 1.9 %convolution_convert_fusion.2 = bf16[192,96]{1,0:T(8,128)(2,1)S(1)} fusion(bf16[192,3584]{1,0:T(8,128)(2,1)} %all-gather.2.cloned.1.call-done, bf16[96,3584]{1,0:T(8,128)(2,1)S(1)} %copy-done), kind=kOutput, calls=%fused_computation.17 | convolution fusion | flops 132139008 | bytes 2101248 | tf_op jit(solution)/shard_map/dot_general | solution.py:53
  59.8 10.8 %fusion.18 = f32[192,2496]{1,0:T(8,128)} fusion(bf16[192,3584]{1,0:T(8,128)(2,1)S(1)} %copy-done.2, bf16[2496,3584]{1,0:T(8,128)(2,1)} %param.10), kind=kOutput, calls=%fused_computation.37 | convolution fusion | flops 3435134976 | bytes 21184512 | tf_op jit(solution)/shard_map/dot_general | solution.py:79
  70.7 4.7 %multiply_convert_fusion = (bf16[192,2496]{1,0:T(8,128)(2,1)}, bf16[192,2496]{1,0:T(8,128)(2,1)}, bf16[192,2496]{1,0:T(8,128)(2,1)S(1)}) fusion(bf16[192,2496]{1,0:T(8,128)(2,1)} %param.8, bf16[192,2496]{1,0:T(8,128)(2,1)} %param.9, f32[192,2496]{1,0:T(8,128)} %fusion.18, bf16[192,96]{1,0:T(8,128)(2,1)S(1)} %convolution_convert_fusion.2, ...), kind=kOutput, calls=%fused_computation.16 | convolution fusion | flops 100638720 | bytes 7225344 | tf_op jit(solution)/shard_map/dot_general | solution.py:82
  75.4 1.3 fusion.19
  76.7 0.4 fusion.20
  77.2 11.6 %psum.7 = bf16[192,96]{1,0:T(8,128)(2,1)S(1)} all-reduce(f32[192,96]{1,0:T(8,128)S(1)} %fusion.20), channel_id=1, replica_groups=mesh['dp'=8,'mp'=4] {'mp'}, use_global_device_ids=true, to_apply=%region_4.5 | all-reduce | flops 18432 | bytes 110592 | tf_op jit(solution)/shard_map/psum | solution.py:52
  88.8 0.2 fusion.21
  89.0 25.9 %fusion = f32[16,896]{1,0:T(8,128)S(1)} fusion(f32[96,896]{1,0:T(8,128)S(1)} %fusion.21), kind=kCustom, calls=%all-reduce-scatter | all-reduce-scatter fusion | flops 114689 | bytes 401920
  114.9 2.4 %collective-permute-start = (f32[16,896]{1,0:T(8,128)S(1)}, f32[16,896]{1,0:T(8,128)S(1)}, u32[]{:S(2)}, u32[]{:S(2)}) collective-permute-start(f32[16,896]{1,0:T(8,128)S(1)} %fusion), channel_id=1, source_target_pairs={{0,4},{4,8},{8,12},{12,16},{16,20},{20,24},{24,28},{1,5},{5,9},{9,... | collective-permute-start | bytes 172040
  117.3 3.2 %collective-permute-start.1 = (f32[12,896]{1,0:T(8,128)S(1)}, f32[12,896]{1,0:T(8,128)S(1)}, u32[]{:S(2)}, u32[]{:S(2)}) collective-permute-start(f32[12,896]{1,0:T(8,128)S(1)} %slice), channel_id=1, source_target_pairs={{0,8},{4,12},{8,16},{12,20},{16,24},{20,28},{1,9},{5,13},{9,17},{1... | collective-permute-start | bytes 129032
  120.5 0.6 fusion.17
  122.4 0.3 concatenate
  122.7 5.7 %all_gather.7 = f32[12,3584]{1,0:T(8,128)S(1)} all-gather(f32[12,896]{1,0:T(8,128)S(1)} %constant_dynamic-slice_fusion), channel_id=1, replica_groups=mesh['dp'=8,'mp'=4] {'mp'}, dimensions={1}, use_global_device_ids=true | all-gather | bytes 215040 | tf_op jit(solution)/shard_map/all_gather | solution.py:78
  128.4 28.2 %all-reduce.5.cloned.1.call-done = f32[2496,96]{0,1:T(8,128)} async-done(((f32[2496,96]{0,1:T(8,128)}), f32[2496,96]{0,1:T(8,128)}) %all-reduce.5.cloned.1.call-update) | async-done | bytes 958480
  156.6 1.7 %dynamic-slice_bitcast_fusion = f32[1,312,96]{1,2,0:T(8,128)} fusion(f32[2496,96]{0,1:T(8,128)} %all-reduce.5.cloned.1.call-done, u32[]{:T(128)S(6)} %multiply.1), kind=kLoop, calls=%fused_computation.18 | loop fusion | bytes 239620 | tf_op jit(solution)/shard_map/broadcast_in_dim | solution.py:89
  158.3 0.7 copy.21
  (23 shorter events, 0.4 us)
Async XLA Ops:
  7.2 50.7 %copy-start = (bf16[96,3584]{1,0:T(8,128)(2,1)S(1)}, bf16[96,3584]{1,0:T(8,128)(2,1)}, u32[]{:S(2)}) copy-start(bf16[96,3584]{1,0:T(8,128)(2,1)} %param.12) | copy-start | bytes 2064388
  9.6 13.7 %all-to-all-start = ((bf16[8,3,1]{1,2,0:T(2,128)(2,1)}), bf16[8,3,1]{1,2,0:T(2,128)(2,1)S(1)}, u32[]{:S(2)}, u32[]{:S(2)}) async-start(bf16[8,3,1]{1,2,0:T(2,128)(2,1)} %convert_element_type.87), calls=%async_computation | async-start | bytes 8192 | tf_op jit(solution)/shard_map/all_to_all | solution.py:35
  23.3 15.3 %all-to-all-start.1 = ((bf16[8,3,7168]{2,1,0:T(4,128)(2,1)}), bf16[8,3,7168]{2,1,0:T(4,128)(2,1)S(1)}, u32[]{:S(2)}, u32[]{:S(2)}) async-start(bf16[8,3,7168]{2,1,0:T(4,128)(2,1)} %all_to_all.13), calls=%async_computation.1 | async-start | bytes 917504 | tf_op jit(solution)/shard_map/all_to_all | solution.py:34
  26.8 31.1 %all-gather.2.cloned.1.call-start = ((), (), s32[]{:S(2)}) async-start(), calls=%async_computation.2 | async-start | bytes 1720320 | tf_op jit(solution)/shard_map/all_gather | solution.py:45
  40.1 116.5 %all-reduce.5.cloned.1.call-start = ((), (), s32[]{:S(2)}) async-start(), calls=%async_computation.3 | async-start | bytes 1966080
  57.9 2.0 %copy-start.2 = (bf16[192,3584]{1,0:T(8,128)(2,1)S(1)}, bf16[192,3584]{1,0:T(8,128)(2,1)}, u32[]{:S(2)}) copy-start(bf16[192,3584]{1,0:T(8,128)(2,1)} %all-gather.2.cloned.1.call-done) | copy-start | bytes 4128772
  59.8 10.8 %copy-start.3 = (bf16[2496,96]{0,1:T(8,128)(2,1)S(1)}, bf16[2496,96]{0,1:T(8,128)(2,1)}, u32[]{:S(2)}) copy-start(bf16[2496,96]{0,1:T(8,128)(2,1)} %param.11) | copy-start | bytes 1437700
  75.4 13.4 %copy-start.1 = (bf16[192,896]{1,0:T(8,128)(2,1)S(1)}, bf16[192,896]{1,0:T(8,128)(2,1)}, u32[]{:S(2)}) copy-start(bf16[192,896]{1,0:T(8,128)(2,1)} %reshape.78) | copy-start | bytes 1032196
  76.7 43.8 %copy-start.4 = (u32[32]{0:T(128)S(1)}, u32[32]{0:T(128)}, u32[]{:S(2)}) copy-start(u32[32]{0:T(128)} %constant.17) | copy-start | bytes 388
  114.9 7.5 %collective-permute-start = (f32[16,896]{1,0:T(8,128)S(1)}, f32[16,896]{1,0:T(8,128)S(1)}, u32[]{:S(2)}, u32[]{:S(2)}) collective-permute-start(f32[16,896]{1,0:T(8,128)S(1)} %fusion), channel_id=1, source_target_pairs={{0,4},{4,8},{8,12},{12,16},{16,20},{20,24},{24,28},{1,5},{5,9},{9,... | collective-permute-start | bytes 172040
  117.3 5.1 %collective-permute-start.1 = (f32[12,896]{1,0:T(8,128)S(1)}, f32[12,896]{1,0:T(8,128)S(1)}, u32[]{:S(2)}, u32[]{:S(2)}) collective-permute-start(f32[12,896]{1,0:T(8,128)S(1)} %slice), channel_id=1, source_target_pairs={{0,8},{4,12},{8,16},{12,20},{16,24},{20,28},{1,9},{5,13},{9,17},{1... | collective-permute-start | bytes 129032
Sparse Core Ops, SparseCore 0:
  40.2 17.5 all-gather.1
  76.9 79.7 all-reduce.4
where the time goes:
time: 166 us
  waiting for transfers between devices  61.4 us (37%)
  blocking collectives  43.2 us (26%)
  matrix products  19.9 us (12%)
  starting transfers between devices  16.4 us (10%)
  between operations  15.5 us (9%)
  local copies, waits for them, and re-layouts  7.48 us (5%)
  other arithmetic  1.9 us (1%)
    unnamed x5, waiting for transfers between devices  28.2 us
    unnamed x1, blocking collectives  25.9 us
    all_gather x1, waiting for transfers between devices, body(): feature_rows = lax.all_gather(packed_tokens, 'mp', axis=1, tiled=True)  17.7 us
    psum x1, blocking collectives, body(): low_rank_rows = lax.psum(low_rank_piece, 'mp').astype(jnp.bfloat16)  11.6 us
    all_to_all x1, waiting for transfers between devices, body(): lax.all_to_all(outgoing, 'dp', split_axis=0, concat_axis=0, tiled=True)  11.4 us
    dot_general x1, matrix products, body(): lax.dot_general(feature_rows, down_weight, (((1,), (1,)), ((), ())), pref...  10.8 us
    all_to_all x1, starting transfers between devices, body(): lax.all_to_all(filled, 'dp', split_axis=0, concat_axis=0, tiled=True)  7.31 us
    all_gather x1, blocking collectives, body(): grad_b_rows = lax.all_gather(part_rows, 'mp', axis=1, tiled=True)  5.69 us
  transfers between devices with their start and end apart: 6, of which 4 were waited for; matrix products, arithmetic and copies ran while one was open for 18% of the time, Pallas kernels for 0%

commit v1 on v0

--- a/solution.py
+++ b/solution.py
@@ -2,6 +2,16 @@
 import jax.numpy as jnp
 from jax import lax
 from jax.sharding import PartitionSpec as P
+
+
+def around_the_ring(x, mesh_axis, dim):
+    n_dev = lax.axis_size(mesh_axis)
+    held, tiles = (x, [x])
+    for _ in range(n_dev - 1):
+        held = lax.ppermute(held, mesh_axis, [(i, (i + 1) % n_dev) for i in range(n_dev)])
+        tiles.insert(0, held)
+    line = jnp.concatenate(tiles, axis=dim)
+    return jnp.roll(line, (lax.axis_index(mesh_axis) + 1) * x.shape[dim], axis=dim)
 
 
 def body(
@@ -42,7 +52,7 @@
         .astype(jnp.bfloat16)
         .reshape(tokens_here, feature_cols)
     )
-    feature_rows = lax.all_gather(packed_tokens, "mp", axis=1, tiled=True)
+    feature_rows = around_the_ring(packed_tokens, "mp", 1)
     gate_vals = gate_preactivation.astype(jnp.float32)
     up_vals = up_preactivation.astype(jnp.float32)
     sigmoid_gate = jax.nn.sigmoid(gate_vals)

time: 166 us -> 162 us (0.976)
  matrix products: 19.9 us -> 14.9 us
  waiting for transfers between devices: 61.4 us -> 64.2 us
    ppermute x0 -> x3, waiting for transfers between devices: none -> 20 us  [around_the_ring(): lax.ppermute(held, mesh_axis, [(i, (i + 1) % n_dev) for i in range(n_dev)])]
    all_gather x1 -> x0, waiting for transfers between devices: 17.7 us -> none  [body(): feature_rows = lax.all_gather(packed_tokens, 'mp', axis=1, tiled=True)]
    dot_general x1, matrix products: 4.7 us -> 0.4 us  [body(): lax.dot_general(passed_through, adapter_first, (((1,), (1,)), ((), ())),...]
    unnamed x5 -> x4, waiting for transfers between devices: 28.2 us -> 28.7 us
  transfers between devices with their start and end apart: 6 -> 8, of which waited for: 4 -> 6; matrix products, arithmetic and copies ran while one was open for 18% -> 17% of each run, Pallas kernels for 0% -> 0%
where the time goes in v1:
time: 162 us; the launch traced here: 161 us
  waiting for transfers between devices  64.2 us (40%)
  blocking collectives  42.2 us (26%)
  between operations  15.6 us (10%)
  starting transfers between devices  15.2 us (9%)
  matrix products  14.9 us (9%)
  local copies, waits for them, and re-layouts  7.45 us (5%)
  other arithmetic  1.9 us (1%)
    unnamed x4, waiting for transfers between devices  28.7 us
    unnamed x1, blocking collectives  24.6 us
    ppermute x3, waiting for transfers between devices, around_the_ring(): lax.ppermute(held, mesh_axis, [(i, (i + 1) % n_dev) for i in range(n_dev)])  20 us
    psum x1, blocking collectives, body(): low_rank_rows = lax.psum(low_rank_piece, 'mp').astype(jnp.bfloat16)  11.5 us
    all_to_all x1, waiting for transfers between devices, body(): lax.all_to_all(outgoing, 'dp', split_axis=0, concat_axis=0, tiled=True)  11.4 us
    dot_general x1, matrix products, body(): lax.dot_general(feature_rows, down_weight, (((1,), (1,)), ((), ())), pref...  11.3 us
    all_to_all x1, starting transfers between devices, body(): lax.all_to_all(filled, 'dp', split_axis=0, concat_axis=0, tiled=True)  7.31 us
    all_gather x1, blocking collectives, body(): grad_b_rows = lax.all_gather(part_rows, 'mp', axis=1, tiled=True)  6.14 us
  transfers between devices with their start and end apart: 8, of which 6 were waited for; matrix products, arithmetic and copies ran while one was open for 17% of the time, Pallas kernels for 0%

profile of v1, /device:TPU:0, one launch (start us, length us, event | category | flops | bytes accessed | tf_op | source)
XLA Modules:
  0.0 161.5 jit_solution(3934705202072427684)
XLA Ops:
  7.2 0.9 convert_reduce_fusion.1
  8.1 0.7 multiply_add_fusion
  8.9 0.7 convert_element_type.87
  9.6 7.3 %all-to-all-start = ((bf16[8,3,1]{1,2,0:T(2,128)(2,1)}), bf16[8,3,1]{1,2,0:T(2,128)(2,1)S(1)}, u32[]{:S(2)}, u32[]{:S(2)}) async-start(bf16[8,3,1]{1,2,0:T(2,128)(2,1)} %convert_element_type.87), calls=%async_computation | async-start | bytes 8192 | tf_op jit(solution)/shard_map/all_to_all | solution.py:45
  16.9 1.1 reshape.77
  18.0 0.2 convolution_convert_fusion.1
  18.3 1.0 all_to_all.13
  19.2 4.1 %all-to-all-done = bf16[8,3,1]{1,2,0:T(2,128)(2,1)S(1)} async-done(((bf16[8,3,1]{1,2,0:T(2,128)(2,1)}), bf16[8,3,1]{1,2,0:T(2,128)(2,1)S(1)}, u32[]{:S(2)}, u32[]{:S(2)}) %all-to-all-start) | async-done | bytes 80 | tf_op jit(solution)/shard_map/all_to_all | solution.py:45
  23.3 3.5 %all-to-all-start.1 = ((bf16[8,3,7168]{2,1,0:T(4,128)(2,1)}), bf16[8,3,7168]{2,1,0:T(4,128)(2,1)S(1)}, u32[]{:S(2)}, u32[]{:S(2)}) async-start(bf16[8,3,7168]{2,1,0:T(4,128)(2,1)} %all_to_all.13), calls=%async_computation.1 | async-start | bytes 917504 | tf_op jit(solution)/shard_map/all_to_all | solution.py:44
  27.2 11.4 %all-to-all-done.1 = bf16[8,3,7168]{2,1,0:T(4,128)(2,1)S(1)} async-done(((bf16[8,3,7168]{2,1,0:T(4,128)(2,1)}), bf16[8,3,7168]{2,1,0:T(4,128)(2,1)S(1)}, u32[]{:S(2)}, u32[]{:S(2)}) %all-to-all-start.1) | async-done | bytes 344096 | tf_op jit(solution)/shard_map/all_to_all | solution.py:44
  38.6 0.3 all_to_all.15
  38.9 0.2 convolution_convert_fusion
  39.4 6.7 %collective-permute-done = bf16[192,896]{1,0:T(8,128)(2,1)S(1)} collective-permute-done((bf16[192,896]{1,0:T(8,128)(2,1)S(1)}, bf16[192,896]{1,0:T(8,128)(2,1)S(1)}, u32[]{:S(2)}, u32[]{:S(2)}) %collective-permute-start) | collective-permute-done | bytes 344096 | tf_op jit(solution)/shard_map/ppermute | solution.py:11
  46.1 6.7 %collective-permute-done.1 = bf16[192,896]{1,0:T(8,128)(2,1)S(1)} collective-permute-done((bf16[192,896]{1,0:T(8,128)(2,1)S(1)}, bf16[192,896]{1,0:T(8,128)(2,1)S(1)}, u32[]{:S(2)}, u32[]{:S(2)}) %collective-permute-start.1) | collective-permute-done | bytes 344096 | tf_op jit(solution)/shard_map/ppermute | solution.py:11
  52.7 6.7 %collective-permute-done.2 = bf16[192,896]{1,0:T(8,128)(2,1)S(1)} collective-permute-done((bf16[192,896]{1,0:T(8,128)(2,1)S(1)}, bf16[192,896]{1,0:T(8,128)(2,1)S(1)}, u32[]{:S(2)}, u32[]{:S(2)}) %collective-permute-start.2) | collective-permute-done | bytes 344096 | tf_op jit(solution)/shard_map/ppermute | solution.py:11
  59.9 0.7 fusion.12
  60.6 0.4 fusion.26
  61.1 0.3 copy-done.4
  61.4 11.3 %multiply_convert_fusion = (bf16[192,2496]{1,0:T(8,128)(2,1)}, bf16[192,2496]{1,0:T(8,128)(2,1)}, bf16[192,2496]{1,0:T(8,128)(2,1)S(1)}) fusion(bf16[192,2496]{1,0:T(8,128)(2,1)S(1)} %copy-done.3, bf16[192,2496]{1,0:T(8,128)(2,1)S(1)} %copy-done.4, f32[192,2496]{1,0:T(8,128)S(1)} %fusion.26, bf16[2496,3584]{1,0:T(8,128)(2,1)} %param.10, ...), kind=kOutput, calls=%fused_computation.16 | convolution fusion | flops 3443761152 | bytes 26075140 | tf_op jit(solution)/shard_map/dot_general | solution.py:89
  72.7 1.3 fusion.27
  74.1 0.4 fusion.28
  74.5 11.5 %psum.7 = bf16[192,96]{1,0:T(8,128)(2,1)S(1)} all-reduce(f32[192,96]{1,0:T(8,128)S(1)} %fusion.28), channel_id=1, replica_groups=mesh['dp'=8,'mp'=4] {'mp'}, use_global_device_ids=true, to_apply=%region_4.5 | all-reduce | flops 18432 | bytes 110592 | tf_op jit(solution)/shard_map/psum | solution.py:62
  86.0 0.2 fusion.29
  86.3 24.6 %fusion = f32[16,896]{1,0:T(8,128)S(1)} fusion(f32[96,896]{1,0:T(8,128)S(1)} %fusion.29), kind=kCustom, calls=%all-reduce-scatter | all-reduce-scatter fusion | flops 114689 | bytes 401920
  110.8 3.1 %collective-permute-start.3 = (f32[16,896]{1,0:T(8,128)S(1)}, f32[16,896]{1,0:T(8,128)S(1)}, u32[]{:S(2)}, u32[]{:S(2)}) collective-permute-start(f32[16,896]{1,0:T(8,128)S(1)} %fusion), channel_id=1, source_target_pairs={{0,4},{4,8},{8,12},{12,16},{16,20},{20,24},{24,28},{1,5},{5,9},{9,... | collective-permute-start | bytes 172040
  113.9 1.3 collective-permute-start.4
  115.2 0.6 fusion.25
  117.1 0.3 concatenate.7
  117.5 6.1 %all_gather.3 = f32[12,3584]{1,0:T(8,128)S(1)} all-gather(f32[12,896]{1,0:T(8,128)S(1)} %constant_dynamic-slice_fusion), channel_id=1, replica_groups=mesh['dp'=8,'mp'=4] {'mp'}, dimensions={1}, use_global_device_ids=true | all-gather | bytes 215040 | tf_op jit(solution)/shard_map/all_gather | solution.py:88
  123.6 28.7 %all-reduce.5.cloned.1.call-done = f32[2496,96]{0,1:T(8,128)} async-done(((f32[2496,96]{0,1:T(8,128)}), f32[2496,96]{0,1:T(8,128)}) %all-reduce.5.cloned.1.call-update) | async-done | bytes 958480
  152.3 1.7 %dynamic-slice_bitcast_fusion = f32[1,312,96]{1,2,0:T(8,128)} fusion(f32[2496,96]{0,1:T(8,128)} %all-reduce.5.cloned.1.call-done, u32[]{:T(128)S(6)} %multiply.1), kind=kLoop, calls=%fused_computation.21 | loop fusion | bytes 239620 | tf_op jit(solution)/shard_map/broadcast_in_dim | solution.py:99
  154.0 0.7 copy.28
  (34 shorter events, 1.2 us)
Async XLA Ops:
  7.2 52.7 %copy-start = (bf16[96,3584]{1,0:T(8,128)(2,1)S(1)}, bf16[96,3584]{1,0:T(8,128)(2,1)}, u32[]{:S(2)}) copy-start(bf16[96,3584]{1,0:T(8,128)(2,1)} %param.12) | copy-start | bytes 2064388
  9.6 13.7 %all-to-all-start = ((bf16[8,3,1]{1,2,0:T(2,128)(2,1)}), bf16[8,3,1]{1,2,0:T(2,128)(2,1)S(1)}, u32[]{:S(2)}, u32[]{:S(2)}) async-start(bf16[8,3,1]{1,2,0:T(2,128)(2,1)} %convert_element_type.87), calls=%async_computation | async-start | bytes 8192 | tf_op jit(solution)/shard_map/all_to_all | solution.py:45
  23.3 15.3 %all-to-all-start.1 = ((bf16[8,3,7168]{2,1,0:T(4,128)(2,1)}), bf16[8,3,7168]{2,1,0:T(4,128)(2,1)S(1)}, u32[]{:S(2)}, u32[]{:S(2)}) async-start(bf16[8,3,7168]{2,1,0:T(4,128)(2,1)} %all_to_all.13), calls=%async_computation.1 | async-start | bytes 917504 | tf_op jit(solution)/shard_map/all_to_all | solution.py:44
  26.8 125.5 %all-reduce.5.cloned.1.call-start = ((), (), s32[]{:S(2)}) async-start(), calls=%async_computation.2 | async-start | bytes 1966080
  39.3 6.7 %collective-permute-start = (bf16[192,896]{1,0:T(8,128)(2,1)S(1)}, bf16[192,896]{1,0:T(8,128)(2,1)S(1)}, u32[]{:S(2)}, u32[]{:S(2)}) collective-permute-start(bf16[192,896]{1,0:T(8,128)(2,1)S(1)} %reshape.78), channel_id=1, source_target_pairs={{0,1},{1,2},{2,3},{3,0},{4,5},{5,6},{6,7},{7,4},{8,9},{9,10},{10,1... | collective-permute-start | bytes 1032200 | tf_op jit(solution)/shard_map/ppermute | solution.py:11
  46.1 6.7 %collective-permute-start.1 = (bf16[192,896]{1,0:T(8,128)(2,1)S(1)}, bf16[192,896]{1,0:T(8,128)(2,1)S(1)}, u32[]{:S(2)}, u32[]{:S(2)}) collective-permute-start(bf16[192,896]{1,0:T(8,128)(2,1)S(1)} %collective-permute-done), channel_id=1, source_target_pairs={{0,1},{1,2},{2,3},{3,0},{4,5},{5,6},{6,7},{7,4},{8,9},{9,10},{10,1... | collective-permute-start | bytes 1032200 | tf_op jit(solution)/shard_map/ppermute | solution.py:11
  52.7 6.7 %collective-permute-start.2 = (bf16[192,896]{1,0:T(8,128)(2,1)S(1)}, bf16[192,896]{1,0:T(8,128)(2,1)S(1)}, u32[]{:S(2)}, u32[]{:S(2)}) collective-permute-start(bf16[192,896]{1,0:T(8,128)(2,1)S(1)} %collective-permute-done.1), channel_id=1, source_target_pairs={{0,1},{1,2},{2,3},{3,0},{4,5},{5,6},{6,7},{7,4},{8,9},{9,10},{10,1... | collective-permute-start | bytes 1032200 | tf_op jit(solution)/shard_map/ppermute | solution.py:11
  59.6 1.1 copy-start.1
  59.8 1.2 copy-start.3
  59.8 1.5 copy-start.4
  72.7 42.5 %copy-start.2 = (u32[32]{0:T(128)S(1)}, u32[32]{0:T(128)}, u32[]{:S(2)}) copy-start(u32[32]{0:T(128)} %constant.43) | copy-start | bytes 388
  110.8 6.3 %collective-permute-start.3 = (f32[16,896]{1,0:T(8,128)S(1)}, f32[16,896]{1,0:T(8,128)S(1)}, u32[]{:S(2)}, u32[]{:S(2)}) collective-permute-start(f32[16,896]{1,0:T(8,128)S(1)} %fusion), channel_id=1, source_target_pairs={{0,4},{4,8},{8,12},{12,16},{16,20},{20,24},{24,28},{1,5},{5,9},{9,... | collective-permute-start | bytes 172040
  113.9 3.2 %collective-permute-start.4 = (f32[12,896]{1,0:T(8,128)S(1)}, f32[12,896]{1,0:T(8,128)S(1)}, u32[]{:S(2)}, u32[]{:S(2)}) collective-permute-start(f32[12,896]{1,0:T(8,128)S(1)} %slice), channel_id=1, source_target_pairs={{0,8},{4,12},{8,16},{12,20},{16,24},{20,28},{1,9},{5,13},{9,17},{1... | collective-permute-start | bytes 129032
Sparse Core Ops, SparseCore 0:
  74.2 78.0 all-reduce.4
